TPU v7x, 32 devices: a whole 2x2x4 slice. The times are simulated.
32 devices in a mesh: grp: 2 (over y), gz: 4 (over z), phi: 4 (over x, core).
Axes of the slice: x: 2, y: 2, z: 4, core: 2. Of those that a mesh axis runs over, the one named last changes fastest.
Arguments:
- charge: bfloat16 [2048, 128, 256], P(('grp', 'phi'), 'gz'), parts along dimension 0, may hold values from -44 to 44
- orders: int32 [64], replicated, may hold values from 1 to 255, as said below
- electrode: int32 [128, 256], P('gz'), may hold values 0 or 1
Outputs:
- distortion: bfloat16 [2048, 128, 256], P(('grp', 'phi'), 'gz'), parts along dimension 0
- potential: float32 [256, 128, 256], P(('grp', 'phi'), 'gz'), parts along dimension 0
There are 2 independent parts, one for each index of `grp`. A program takes and returns all parts, laid end to end along the dimension named above; an argument that names none is the same for every part. Nothing has to cross between parts.
Inputs may be any that keep to these rules, and one draw needn't show every extreme that they name: The 64 orders are distinct, and 1 and 255 are among them.
All inputs are finite; a program needn't handle non-finite values. No bound on the sum of `electrode` on one device may be relied on, other than what follows from the above.
Results may differ from a plain program's by a relative error of at most 0.0059.
Values may be sent and summed in bfloat16 or wider, within the bound.
No kernel may reach another device: no remote copies, remote signals or barrier semaphores. Data moves between devices by JAX's collectives and lax.ppermute only.
A program may use at most 64 MiB of HBM per device.

v0:
```python
import math

import jax
import jax.numpy as jnp
from jax import lax
from jax.sharding import PartitionSpec as P

PHI = 1024
ORDERS = 64
MODES = 128
SWEEPS = 4


def with_halo(array, sides, width):
    for axis, dim in sides:
        count, length = (lax.axis_size(axis), array.shape[dim])
        up = [(i, (i + 1) % count) for i in range(count - 1)]
        down = [(j, i) for i, j in up]
        last = lax.slice_in_dim(array, length - width, length, axis=dim)
        first = lax.slice_in_dim(array, 0, width, axis=dim)
        before = lax.ppermute(last, axis, up)
        after = lax.ppermute(first, axis, down)
        array = jnp.concatenate([before, array, after], axis=dim)
    return array


def passed_along(block, axis, distance):
    devices = range(lax.axis_size(axis))
    route = [(i - distance, i) for i in devices if i - distance in devices]
    return lax.ppermute(block, axis, route)


def make_table(orders):
    positions = jnp.arange(PHI, dtype=jnp.int32)
    phase_int = orders[:, None] * positions[None, :] % PHI
    angles = phase_int.astype(jnp.float32) * (2.0 * math.pi / PHI)
    return jnp.concatenate([jnp.cos(angles), jnp.sin(angles)], 0).astype(jnp.bfloat16)


def radial_terms(order_values, radial_cells):
    radius = jnp.arange(radial_cells, dtype=jnp.float32) + (radial_cells // 2 + 0.5)
    outer_coef = 1.0 + 0.5 / radius
    inner_coef = 1.0 - 0.5 / radius
    diagonal = 4.0 + (order_values[:, None] / radius[None, :]) ** 2
    return (outer_coef, inner_coef, diagonal[:, None, :])


def radial_sum(field_now, outer_coef, inner_coef):
    zero_plane = jnp.zeros_like(field_now[..., :1])
    upper_cell = jnp.concatenate([field_now[..., 1:], zero_plane], -1)
    lower_cell = jnp.concatenate([zero_plane, field_now[..., :-1]], -1)
    return (outer_coef * upper_cell + inner_coef * lower_cell, upper_cell, lower_cell)


def on_device(charge, orders, electrode):
    phi_rows, slab_depth, radial_cells = charge.shape
    mode_rows = MODES // lax.axis_size("phi")
    slab_count = lax.axis_size("gz")
    basis_table = make_table(orders)
    local_cols = lax.dynamic_slice_in_dim(
        basis_table, lax.axis_index("phi") * phi_rows, phi_rows, 1
    )
    flattened = charge.reshape(phi_rows, slab_depth * radial_cells)
    summed = lax.psum_scatter(
        jnp.dot(local_cols, flattened, preferred_element_type=jnp.float32),
        "phi",
        scatter_dimension=0,
        tiled=True,
    )
    source = summed.reshape(mode_rows, slab_depth, radial_cells) * PHI ** (-0.5)
    mode_ids = lax.axis_index("phi") * mode_rows + jnp.arange(mode_rows, dtype=jnp.int32)
    matches = mode_ids[:, None] % ORDERS == jnp.arange(ORDERS, dtype=jnp.int32)[None, :]
    order_values = jnp.sum(jnp.where(matches, orders[None, :], 0), 1).astype(jnp.float32)
    outer_coef, inner_coef, diagonal = radial_terms(order_values, radial_cells)
    open_cells = (1 - electrode).astype(jnp.float32)
    stacked = jnp.concatenate([source, open_cells[None]], 0)
    widened = with_halo(stacked, (("gz", 1),), SWEEPS)
    wide_source = widened[:mode_rows]
    wide_open = widened[mode_rows]
    potential = wide_open * wide_source / diagonal
    for sweep in range(SWEEPS):
        zero_plane = jnp.zeros_like(potential[:, :1])
        upper_plane = jnp.concatenate([potential[:, 1:], zero_plane], 1)
        lower_plane = jnp.concatenate([zero_plane, potential[:, :-1]], 1)
        radial, _, _ = radial_sum(potential, outer_coef, inner_coef)
        neighbours = upper_plane + lower_plane + radial
        potential = wide_open * (wide_source + neighbours) / diagonal
    potential = potential[:, SWEEPS : SWEEPS + slab_depth]
    _, upper_cell, lower_cell = radial_sum(potential, outer_coef, inner_coef)
    radial_field = 0.5 * (upper_cell - lower_cell)
    local_sum = lax.cumsum(radial_field, axis=1, reverse=True)
    totals = local_sum[:, 0]

    def relay(step_index, incoming):
        return passed_along(totals + incoming, "gz", -1)

    incoming = lax.fori_loop(0, slab_count - 1, relay, jnp.zeros_like(totals))
    mode_shift = ((local_sum + incoming[:, None, :]) * (slab_count * slab_depth) ** (-0.5)).astype(
        jnp.bfloat16
    )
    weights_all = local_cols.T
    shard_piece = lax.all_gather(mode_shift, "phi", axis=0, tiled=True)
    row_count = shard_piece.shape[0]
    running = jnp.dot(
        weights_all,
        shard_piece.reshape(row_count, slab_depth * radial_cells),
        preferred_element_type=jnp.float32,
    )
    distortion = (
        (running * MODES ** (-0.5)).astype(jnp.bfloat16).reshape(phi_rows, slab_depth, radial_cells)
    )
    return (distortion, potential)


def solution(mesh):
    return jax.shard_map(
        on_device,
        mesh=mesh,
        in_specs=(P(("grp", "phi"), "gz", None), P(), P("gz", None)),
        out_specs=(P(("grp", "phi"), "gz", None), P(("grp", "phi"), "gz", None)),
        check_vma=False,
    )
```

profile of v0, /device:TPU:0, one launch (start us, length us, event | category | flops | bytes accessed | tf_op | source)
XLA Modules:
  0.0 145.1 jit_solution(1187935521183579783)
XLA Ops:
  7.2 0.0 reduce-scatter.2.cloned.1.call-start
  7.2 1.9 %sine_convert_fusion = (bf16[64,1024]{1,0:T(8,128)(2,1)S(1)}, bf16[64,1024]{1,0:T(8,128)(2,1)S(1)}) fusion(s32[64]{0:T(128)} %param.6), kind=kLoop, calls=%fused_computation.23 | loop fusion | flops 1048576 | bytes 262400 | tf_op jit(solution)/shard_map/convert.1
  9.1 8.5 %copy.10 = bf16[32,8,32,256]{3,1,2,0:T(8,128)(2,1)} copy(bf16[32,8,32,256]{3,2,1,0:T(8,128)(2,1)} %bitcast.25) | data formatting | bytes 8388608
  17.6 4.9 %fusion.12 = f32[128,8192]{1,0:T(8,128)} fusion(bf16[256,8192]{1,0:T(8,128)(2,1)} %bitcast.22, s32[]{:T(128)S(6)} %select_n.26, bf16[64,1024]{1,0:T(8,128)(2,1)S(1)} %get-tuple-element.47, bf16[64,1024]{1,0:T(8,128)(2,1)S(1)} %get-tuple-element.46), kind=kOutput, calls=%fused_computation.46 | convolution fusion | flops 537001984 | bytes 8650756 | tf_op jit(solution)/shard_map/dot_general | solution.py:65
  22.5 0.0 copy-start.1
  22.5 0.0 reduce-scatter.2.cloned.1.call-update
  22.5 0.0 all-gather.2.cloned.1.call-start
  22.6 0.6 copy-done.1
  23.1 0.2 select_reduce_fusion
  23.3 0.0 copy-done
  23.3 46.6 %reduce-scatter.2.cloned.1.call-done = f32[32,8192]{1,0:T(8,128)} async-done(((f32[128,8192]{1,0:T(8,128)}), f32[32,8192]{1,0:T(8,128)}) %reduce-scatter.2.cloned.1.call-update) | async-done | bytes 1048592 | tf_op jit(solution)/shard_map/reduce_scatter | solution.py:64
  70.0 1.3 broadcast_multiply_fusion
  71.3 0.3 copy.11
  71.6 3.4 %collective-permute-start.1 = (f32[33,4,256]{2,1,0:T(4,128)S(1)}, f32[33,4,256]{2,1,0:T(4,128)S(1)}, u32[]{:S(2)}, u32[]{:S(2)}) collective-permute-start(f32[33,4,256]{2,1,0:T(4,128)S(1)} %get-tuple-element.44), channel_id=1, source_target_pairs={{0,4},{4,8},{8,12},{1,5},{5,9},{9,13},{2,6},{6,10},{10,14},{3,7},{... | collective-permute-start | bytes 405512 | tf_op jit(solution)/shard_map/ppermute | solution.py:21
  75.0 1.5 %collective-permute-start.2 = (f32[33,4,256]{2,1,0:T(4,128)S(1)}, f32[33,4,256]{2,1,0:T(4,128)S(1)}, u32[]{:S(2)}, u32[]{:S(2)}) collective-permute-start(f32[33,4,256]{2,1,0:T(4,128)S(1)} %get-tuple-element.45), channel_id=1, source_target_pairs={{4,0},{8,4},{12,8},{5,1},{9,5},{13,9},{6,2},{10,6},{14,10},{7,3},{... | collective-permute-start | bytes 405512 | tf_op jit(solution)/shard_map/ppermute | solution.py:22
  76.5 0.1 fusion.10
  76.6 1.1 collective-permute-done.1
  77.7 4.3 %collective-permute-done.2 = f32[33,4,256]{2,1,0:T(4,128)S(1)} collective-permute-done((f32[33,4,256]{2,1,0:T(4,128)S(1)}, f32[33,4,256]{2,1,0:T(4,128)S(1)}, u32[]{:S(2)}, u32[]{:S(2)}) %collective-permute-start.2) | collective-permute-done | bytes 135200 | tf_op jit(solution)/shard_map/ppermute | solution.py:22
  82.0 0.3 multiply_divide_fusion.4
  82.2 0.4 fusion.23
  82.7 0.2 fusion.22
  82.9 0.9 multiply_divide_fusion.3
  83.8 0.4 fusion.21
  84.2 0.2 fusion.20
  84.4 0.9 multiply_divide_fusion.2
  85.3 0.4 fusion.19
  85.7 0.2 fusion.18
  85.9 0.9 multiply_divide_fusion.1
  86.8 0.4 fusion.17
  87.2 0.2 fusion.16
  87.5 0.9 multiply_divide_fusion
  88.3 0.4 fusion.15
  88.7 0.3 subtract_multiply_fusion
  89.1 1.0 fusion.1
  90.1 17.4 %while.10 = (s32[]{:T(128)}, f32[32,256]{1,0:T(8,128)S(1)}, f32[32,256]{1,0:T(8,128)S(1)}, s32[]{:T(128)}) while((s32[]{:T(128)}, f32[32,256]{1,0:T(8,128)S(1)}, f32[32,256]{1,0:T(8,128)S(1)}, s32[]{:T(128)}) %tuple.34), condition=%wide.region_4.5_spmd, body=%wide.region_3.4_spmd.sunk | while | flops 8194 | bytes 229469 | solution.py:97
  90.1 1.3 collective-permute-start
  91.5 4.5 %collective-permute-done = f32[32,256]{1,0:T(8,128)S(1)} collective-permute-done((f32[32,256]{1,0:T(8,128)S(1)}, f32[32,256]{1,0:T(8,128)S(1)}, u32[]{:S(2)}, u32[]{:S(2)}) %collective-permute-start) | collective-permute-done | bytes 32800 | tf_op jit(solution)/shard_map/while/body/eval_jaxpr/ppermute | solution.py:30
  96.0 1.3 collective-permute-start
  97.3 4.5 %collective-permute-done = f32[32,256]{1,0:T(8,128)S(1)} collective-permute-done((f32[32,256]{1,0:T(8,128)S(1)}, f32[32,256]{1,0:T(8,128)S(1)}, u32[]{:S(2)}, u32[]{:S(2)}) %collective-permute-start) | collective-permute-done | bytes 32800 | tf_op jit(solution)/shard_map/while/body/eval_jaxpr/ppermute | solution.py:30
  101.8 1.3 collective-permute-start
  103.1 4.5 %collective-permute-done = f32[32,256]{1,0:T(8,128)S(1)} collective-permute-done((f32[32,256]{1,0:T(8,128)S(1)}, f32[32,256]{1,0:T(8,128)S(1)}, u32[]{:S(2)}, u32[]{:S(2)}) %collective-permute-start) | collective-permute-done | bytes 32800 | tf_op jit(solution)/shard_map/while/body/eval_jaxpr/ppermute | solution.py:30
  107.6 0.9 multiply_convert_fusion
  108.5 0.0 all-gather.2.cloned.1.call-update
  108.5 1.1 slice.117
  109.6 20.7 %all-gather.2.cloned.1.call-done = bf16[128,32,256]{2,0,1:T(8,128)(2,1)} async-done(((bf16[32,32,256]{2,0,1:T(8,128)(2,1)}), bf16[128,32,256]{2,0,1:T(8,128)(2,1)}) %all-gather.2.cloned.1.call-update) | async-done | bytes 2097168 | tf_op jit(solution)/shard_map/all_gather | solution.py:102
  130.3 3.2 %copy.9 = bf16[128,32,256]{0,2,1:T(8,128)(2,1)S(1)} copy(bf16[128,32,256]{2,0,1:T(8,128)(2,1)} %all-gather.2.cloned.1.call-done) | data formatting | bytes 4194304 | tf_op jit(solution)/shard_map/all_gather | solution.py:102
  133.5 1.3 fusion
  134.8 3.4 %copy.12 = bf16[32,8,32,256]{3,2,1,0:T(8,128)(2,1)} copy(bf16[32,8,32,256]{3,1,2,0:T(8,128)(2,1)S(1)} %bitcast.23) | data formatting | bytes 8388608
  (13 shorter events, 0.1 us)
Async XLA Ops:
  7.2 62.8 %reduce-scatter.2.cloned.1.call-start = ((), (), s32[]{:S(2)}) async-start(), calls=%async_computation.1 | async-start | bytes 5242880 | tf_op jit(solution)/shard_map/reduce_scatter | solution.py:64
  22.5 0.7 copy-start.1
  22.5 0.9 copy-start
  22.5 107.8 %all-gather.2.cloned.1.call-start = ((), (), s32[]{:S(2)}) async-start(), calls=%async_computation.2 | async-start | bytes 2621440 | tf_op jit(solution)/shard_map/all_gather | solution.py:102
  71.6 6.1 %collective-permute-start.1 = (f32[33,4,256]{2,1,0:T(4,128)S(1)}, f32[33,4,256]{2,1,0:T(4,128)S(1)}, u32[]{:S(2)}, u32[]{:S(2)}) collective-permute-start(f32[33,4,256]{2,1,0:T(4,128)S(1)} %get-tuple-element.44), channel_id=1, source_target_pairs={{0,4},{4,8},{8,12},{1,5},{5,9},{9,13},{2,6},{6,10},{10,14},{3,7},{... | collective-permute-start | bytes 405512 | tf_op jit(solution)/shard_map/ppermute | solution.py:21
  75.0 6.9 %collective-permute-start.2 = (f32[33,4,256]{2,1,0:T(4,128)S(1)}, f32[33,4,256]{2,1,0:T(4,128)S(1)}, u32[]{:S(2)}, u32[]{:S(2)}) collective-permute-start(f32[33,4,256]{2,1,0:T(4,128)S(1)} %get-tuple-element.45), channel_id=1, source_target_pairs={{4,0},{8,4},{12,8},{5,1},{9,5},{13,9},{6,2},{10,6},{14,10},{7,3},{... | collective-permute-start | bytes 405512 | tf_op jit(solution)/shard_map/ppermute | solution.py:22
  90.1 5.8 %collective-permute-start = (f32[32,256]{1,0:T(8,128)S(1)}, f32[32,256]{1,0:T(8,128)S(1)}, u32[]{:S(2)}, u32[]{:S(2)}) collective-permute-start(f32[32,256]{1,0:T(8,128)S(1)} %add.264), channel_id=1, source_target_pairs={{4,0},{8,4},{12,8},{5,1},{9,5},{13,9},{6,2},{10,6},{14,10},{7,3},{... | collective-permute-start | bytes 98312 | tf_op jit(solution)/shard_map/while/body/eval_jaxpr/ppermute | solution.py:30
  96.0 5.8 %collective-permute-start = (f32[32,256]{1,0:T(8,128)S(1)}, f32[32,256]{1,0:T(8,128)S(1)}, u32[]{:S(2)}, u32[]{:S(2)}) collective-permute-start(f32[32,256]{1,0:T(8,128)S(1)} %add.264), channel_id=1, source_target_pairs={{4,0},{8,4},{12,8},{5,1},{9,5},{13,9},{6,2},{10,6},{14,10},{7,3},{... | collective-permute-start | bytes 98312 | tf_op jit(solution)/shard_map/while/body/eval_jaxpr/ppermute | solution.py:30
  101.8 5.8 %collective-permute-start = (f32[32,256]{1,0:T(8,128)S(1)}, f32[32,256]{1,0:T(8,128)S(1)}, u32[]{:S(2)}, u32[]{:S(2)}) collective-permute-start(f32[32,256]{1,0:T(8,128)S(1)} %add.264), channel_id=1, source_target_pairs={{4,0},{8,4},{12,8},{5,1},{9,5},{13,9},{6,2},{10,6},{14,10},{7,3},{... | collective-permute-start | bytes 98312 | tf_op jit(solution)/shard_map/while/body/eval_jaxpr/ppermute | solution.py:30
Sparse Core Ops, SparseCore 0:
  22.6 47.3 reduce-scatter.1
  108.6 21.6 all-gather.1
where the time goes:
time: 146 us; the launch traced here: 145 us
  waiting for transfers between devices  86.2 us (59%)
  local copies, waits for them, and re-layouts  20.1 us (14%)
  between operations  14.3 us (10%)
  other arithmetic  9.56 us (7%)
  starting transfers between devices  8.8 us (6%)
  matrix products  6.15 us (4%)
    reduce_scatter x1, waiting for transfers between devices, on_device(): lax.psum_scatter(jnp.dot(local_cols, flattened, preferred_element_type=jn...  46.6 us
    all_gather x1, waiting for transfers between devices, on_device(): shard_piece = lax.all_gather(mode_shift, 'phi', axis=0, tiled=True)  20.7 us
    ppermute x3, waiting for transfers between devices, passed_along(): return lax.ppermute(block, axis, route)  13.5 us
    unnamed x7, local copies, waits for them, and re-layouts  12.8 us
    dot_general x1, matrix products, on_device(): jnp.dot(local_cols, flattened, preferred_element_type=jnp.float32)  4.86 us
    ppermute x1, waiting for transfers between devices, with_halo(): after = lax.ppermute(first, axis, down)  4.26 us
    ppermute x3, starting transfers between devices, passed_along(): return lax.ppermute(block, axis, route)  3.85 us
    div x4, other arithmetic, on_device(): potential = wide_open * (wide_source + neighbours) / diagonal  3.47 us
  transfers between devices with their start and end apart: 7, of which 7 were waited for; matrix products, arithmetic and copies ran while one was open for 1% of the time, Pallas kernels for 0%

commit v1 on v0

v1 whole, which is shorter than its diff:
```python
import functools
import math

import jax
import jax.numpy as jnp
from jax import lax
from jax.experimental import pallas as pl
from jax.experimental.pallas import tpu as pltpu
from jax.sharding import PartitionSpec as P

PHI = 1024
ORDERS = 64
MODES = 128
SWEEPS = 4
TILE = 8
LANES = 128
F32 = jnp.float32
BF16 = jnp.bfloat16


def params():
    return pltpu.CompilerParams(vmem_limit_bytes=48 << 20)


def cosine(phase):
    folded = jnp.abs(jnp.bitwise_and(phase, PHI - 1) - PHI // 2)
    sign = jnp.where(folded > PHI // 4, 1.0, -1.0).astype(F32)
    near = jnp.where(folded > PHI // 4, PHI // 2 - folded, folded)
    angle = near.astype(F32) * (2.0 * math.pi / PHI)
    square = angle * angle
    total = jnp.full_like(square, 1.0 / math.factorial(14) * -1.0)
    for term in range(6, -1, -1):
        total = total * square + (-1.0) ** term / math.factorial(2 * term)
    return sign * total


def reversed_bits(count):
    order, step = [0], count
    while step > 1:
        step //= 2
        order = order + [g + step for g in order]
    return order


def roll(value, shift):
    return pltpu.roll(value, shift % value.shape[-1], value.ndim - 1)


def analyse_kernel(charge_ref, basis_ref, keep_ref, send_ref, staged):
    rows, depth, cells = charge_ref.shape
    half = keep_ref.shape[1]
    parts = range(0, cells, LANES)
    for i, lane in enumerate(parts):
        block = charge_ref[:, :, lane:lane + LANES].astype(F32)
        staged[i] = block.reshape(rows * depth, LANES)
    for z in range(depth):
        planes = [staged[i, pl.ds(z, rows, stride=depth), :] for i, _ in enumerate(parts)]
        plane = jnp.concatenate(planes, 1).astype(BF16)
        sums = jnp.dot(basis_ref[...], plane, preferred_element_type=F32)
        keep_ref[z] = sums[:half]
        send_ref[z] = sums[half:]


def analyse(charge, basis, tiles):
    rows, depth, cells = charge.shape
    modes = basis.shape[0]
    first, step = tiles[0], (tiles[1] - tiles[0] if len(tiles) > 1 else 1)
    part = jax.ShapeDtypeStruct((len(tiles) * TILE, modes // 2, cells), F32)
    out = pl.BlockSpec((TILE, modes // 2, cells), lambda i: (i, 0, 0))
    return pl.pallas_call(
        analyse_kernel,
        grid=(len(tiles),),
        in_specs=[
            pl.BlockSpec((rows, TILE, cells), lambda i: (0, first + step * i, 0)),
            pl.BlockSpec((modes, rows), lambda i: (0, 0)),
        ],
        out_specs=[out, out],
        out_shape=[part, part],
        scratch_shapes=[pltpu.VMEM((cells // LANES, rows * TILE, LANES), F32)],
        compiler_params=params(),
        name="analyse",
    )(charge, basis)


def round_kernel(order, reset, keep_ref, recv_ref, state_ref, out_ref, left_ref):
    error = state_ref[...]
    for z in order:
        if z in reset:
            error = jnp.zeros_like(error)
        exact = keep_ref[z] + recv_ref[z] + error
        rounded = exact.astype(BF16)
        out_ref[z] = rounded
        error = exact - rounded.astype(F32)
    left_ref[...] = error


def round_sums(keep, recv, state, order, reset):
    depth, modes, cells = keep.shape
    rows = modes // 2
    part = pl.BlockSpec((depth, rows, cells), lambda i: (0, 1, 0))
    flat = pl.BlockSpec((rows, cells), lambda i: (0, 0))
    return pl.pallas_call(
        functools.partial(round_kernel, order, reset),
        grid=(1,),
        in_specs=[part, part, flat],
        out_specs=[pl.BlockSpec((depth, rows, cells), lambda i: (0, 0, 0)), flat],
        out_shape=[
            jax.ShapeDtypeStruct((depth, rows, cells), BF16),
            jax.ShapeDtypeStruct((rows, cells), F32),
        ],
        compiler_params=params(),
        name="round_sums",
    )(keep, recv, state)


def solve_kernel(depth, total_depth, keep_ref, recv_ref, far_ref, before_ref, after_ref,
                 open_ref, order_ref, pot_ref, shift_ref, total_ref, src, pot, staged):
    rows, cells = before_ref.shape[1:]
    parts = range(0, cells, LANES)
    halo = SWEEPS
    column = lax.broadcasted_iota(jnp.int32, (rows, cells), 1)
    radius = column.astype(F32) + (cells // 2 + 0.5)
    outer = jnp.where(column == cells - 1, 0.0, 1.0 + 0.5 / radius)
    inner = jnp.where(column == 0, 0.0, 1.0 - 0.5 / radius)
    ratio = order_ref[...] / radius
    inverse = 1.0 / (4.0 + ratio * ratio)
    scale = PHI ** -0.5
    src[0:halo] = before_ref[...]
    src[halo + depth:] = after_ref[...]

    def gather(z, carry):
        src[z + halo] = (keep_ref[z] + recv_ref[z] + far_ref[z].astype(F32)) * scale
        return carry

    lax.fori_loop(0, depth, gather, 0, unroll=4)
    span = depth + 2 * halo

    def start(z, carry):
        pot[z] = src[z] * inverse * open_ref[pl.ds(z, 1), :]
        return carry

    lax.fori_loop(0, span, start, 0, unroll=4)

    def updated(z, here, below, above):
        radial = outer * roll(here, -1) + inner * roll(here, 1)
        return (src[z] + (below + above) + radial) * inverse * open_ref[pl.ds(z, 1), :]

    for sweep in range(1, SWEEPS):
        def step(z, below):
            here = pot[z]
            pot[z] = updated(z, here, below, pot[z + 1])
            return here

        lax.fori_loop(sweep, span - sweep, step, pot[sweep - 1], unroll=2)

    field_scale = 0.5 * total_depth ** -0.5
    upper_scale = jnp.where(column == cells - 1, 0.0, field_scale)
    lower_scale = jnp.where(column == 0, 0.0, field_scale)

    def last(i, carry):
        above, running = carry
        z = depth - 1 - i
        here = pot[z + halo]
        new = updated(z + halo, here, pot[z + halo - 1], above)
        for i, lane in enumerate(parts):
            staged[i, pl.ds(z, rows, stride=depth), :] = new[:, lane:lane + LANES]
        running = running + (upper_scale * roll(new, -1) - lower_scale * roll(new, 1))
        shift_ref[z] = running
        return here, running

    _, running = lax.fori_loop(0, depth, last, (pot[depth + halo], jnp.zeros((rows, cells), F32)), unroll=2)
    total_ref[...] = running
    for i, lane in enumerate(parts):
        pot_ref[:, :, lane:lane + LANES] = staged[i].reshape(rows, depth, LANES)


def solve(keep, recv, far, before, after, open_cells, orders, total_depth):
    depth, _, cells = keep.shape
    rows = far.shape[1]
    span = depth + 2 * SWEEPS
    half = pl.BlockSpec((depth, rows, cells), lambda i: (0, 0, 0))
    edge = pl.BlockSpec((SWEEPS, rows, cells), lambda i: (0, 0, 0))
    flat = lambda a, b: pl.BlockSpec((a, b), lambda i: (0, 0))
    return pl.pallas_call(
        functools.partial(solve_kernel, depth, total_depth),
        grid=(1,),
        in_specs=[half, half, half, edge, edge, flat(span, cells), flat(rows, 1)],
        out_specs=[pl.BlockSpec((rows, depth, cells), lambda i: (0, 0, 0)), half, flat(rows, cells)],
        out_shape=[
            jax.ShapeDtypeStruct((rows, depth, cells), F32),
            jax.ShapeDtypeStruct((depth, rows, cells), F32),
            jax.ShapeDtypeStruct((rows, cells), F32),
        ],
        scratch_shapes=[
            pltpu.VMEM((span, rows, cells), F32),
            pltpu.VMEM((span, rows, cells), F32),
            pltpu.VMEM((cells // LANES, rows * depth, LANES), F32),
        ],
        compiler_params=params(),
        name="solve",
    )(keep, recv, far, before, after, open_cells, orders)


def synthesise_kernel(count, *refs):
    pieces, weight_ref, out_ref, staged = refs[:count], refs[count], refs[count + 1], refs[count + 2]
    rows, depth, cells = out_ref.shape
    parts = range(0, cells, LANES)
    for z in range(depth):
        shifts = jnp.concatenate([piece[z] for piece in pieces], 0)
        plane = jnp.dot(weight_ref[...], shifts, preferred_element_type=F32) * MODES ** -0.5
        for i, lane in enumerate(parts):
            staged[i, pl.ds(z, rows, stride=depth), :] = plane[:, lane:lane + LANES]
    for i, lane in enumerate(parts):
        out_ref[:, :, lane:lane + LANES] = staged[i].reshape(rows, depth, LANES).astype(BF16)


def synthesise(pieces, weights):
    depth, _, cells = pieces[0].shape
    rows, modes = weights.shape
    return pl.pallas_call(
        functools.partial(synthesise_kernel, len(pieces)),
        grid=(depth // TILE,),
        in_specs=[pl.BlockSpec((TILE, piece.shape[1], cells), lambda i: (i, 0, 0)) for piece in pieces]
        + [pl.BlockSpec((rows, modes), lambda i: (0, 0))],
        out_specs=pl.BlockSpec((rows, TILE, cells), lambda i: (0, i, 0)),
        out_shape=jax.ShapeDtypeStruct((rows, depth, cells), BF16),
        scratch_shapes=[pltpu.VMEM((cells // LANES, rows * TILE, LANES), F32)],
        compiler_params=params(),
        name="synthesise",
    )(*pieces, weights)


def exchanged(block, axis, bit):
    return lax.ppermute(block, axis, [(i, i ^ bit) for i in range(lax.axis_size(axis))])


def moved(block, axis, distance):
    devices = range(lax.axis_size(axis))
    return lax.ppermute(block, axis, [(i - distance, i) for i in devices if i - distance in devices])


def later_sum(totals, axis):
    count = lax.axis_size(axis)
    if count <= 4:
        arrived = [moved(totals, axis, -d) for d in range(1, count)]
        return sum(arrived[1:], arrived[0])
    running, step = totals, 1
    while step < count:
        running = running + moved(running, axis, -step)
        step *= 2
    return moved(running, axis, -1)


def on_device(charge, orders, electrode):
    phi_rows, depth, cells = charge.shape
    devices = lax.axis_size("phi")
    mode_rows = MODES // devices
    total_depth = lax.axis_size("gz") * depth
    me = lax.axis_index("phi")
    groups = reversed_bits(devices)

    group_of_row = jnp.array([g for g in groups for _ in range(mode_rows)], jnp.int32)
    row_in_group = jnp.array([i for _ in groups for i in range(mode_rows)], jnp.int32)
    mode_ids = jnp.bitwise_xor(group_of_row, me) * mode_rows + row_in_group
    matches = mode_ids[:, None] % ORDERS == jnp.arange(ORDERS, dtype=jnp.int32)[None, :]
    row_orders = jnp.sum(jnp.where(matches, orders[None, :], 0), 1)
    quarter = jnp.where(mode_ids >= ORDERS, PHI // 4, 0)
    cells_here = me * phi_rows + jnp.arange(phi_rows, dtype=jnp.int32)
    basis = cosine(row_orders[:, None] * cells_here[None, :] - quarter[:, None]).astype(BF16)
    weights = cosine(cells_here[:, None] * row_orders[None, :] - quarter[None, :]).astype(BF16)

    open_cells = (1 - electrode).astype(F32)
    open_wide = jnp.concatenate(
        [moved(open_cells[depth - SWEEPS:], "gz", 1), open_cells, moved(open_cells[:SWEEPS], "gz", -1)], 0
    )

    keep, send = analyse(charge, basis, list(range(depth // TILE)))
    bit = 1
    recv = exchanged(send, "phi", bit)
    while bit * 4 < devices:
        bit *= 2
        half = keep.shape[1] // 2
        joined = keep + recv
        keep = joined[:, :half]
        recv = exchanged(joined[:, half:], "phi", bit)
    top = devices // 2
    state = jnp.zeros((mode_rows, cells), F32)
    far, _ = round_sums(keep, recv, state, list(range(depth - 1, -1, -1)), ())
    far = exchanged(far, "phi", top)
    scale = PHI ** -0.5

    def edge(a, b):
        return (keep[a:b, :mode_rows] + recv[a:b, :mode_rows] + far[a:b].astype(F32)) * scale

    before = moved(edge(depth - SWEEPS, depth), "gz", 1)
    after = moved(edge(0, SWEEPS), "gz", -1)
    own_orders = row_orders[:mode_rows].astype(F32)[:, None]
    potential, shift, totals = solve(keep, recv, far, before, after, open_wide, own_orders, total_depth)
    incoming = later_sum(totals, "gz")
    pieces = [(shift + incoming[None]).astype(BF16)]
    bit = top
    while bit:
        pieces = pieces + [exchanged(piece, "phi", bit) for piece in pieces]
        bit //= 2
    distortion = synthesise(pieces, weights)
    return distortion, potential


def solution(mesh):
    return jax.shard_map(
        on_device,
        mesh=mesh,
        in_specs=(P(("grp", "phi"), "gz", None), P(), P("gz", None)),
        out_specs=(P(("grp", "phi"), "gz", None), P(("grp", "phi"), "gz", None)),
        check_vma=False,
    )
```

time: 146 us -> 73.9 us (0.51)
  waiting for transfers between devices: 86.2 us -> 29.3 us
  Pallas kernels: 0 us -> 20.2 us
  local copies, waits for them, and re-layouts: 20.1 us -> 1.69 us
  between operations: 14.3 us -> 0.78 us
  starting transfers between devices: 8.8 us -> 19.5 us
  other arithmetic: 9.56 us -> 2.07 us
  matrix products: 6.15 us -> 0 us
    reduce_scatter x1 -> x0, waiting for transfers between devices: 46.6 us -> none  [on_device(): lax.psum_scatter(jnp.dot(local_cols, flattened, preferred_element_type=jn...]
    all_gather x1 -> x0, waiting for transfers between devices: 20.7 us -> none  [on_device(): shard_piece = lax.all_gather(mode_shift, 'phi', axis=0, tiled=True)]
    pallas_call x0 -> x4, Pallas kernels: none -> 20.2 us  [the longest x1 10.8 us: solve(): pl.pallas_call(functools.partial(solve_kernel, depth, total_depth), grid=...]
    unnamed x7 -> x6, local copies, waits for them, and re-layouts: 12.8 us -> 1.6 us
    ppermute x5 -> x12, starting transfers between devices: 8.72 us -> 19.5 us  [the longest x7 14.5 us: moved(): lax.ppermute(block, axis, [(i - distance, i) for i in devices if i - dist...]
    ppermute x5 -> x12, waiting for transfers between devices: 18.9 us -> 29.3 us  [the longest x5 22.2 us: exchanged(): lax.ppermute(block, axis, [(i, i ^ bit) for i in range(lax.axis_size(axis...]
    dot_general x2 -> x0, matrix products: 6.15 us -> none  [the longest x1 4.86 us: on_device(): jnp.dot(local_cols, flattened, preferred_element_type=jnp.float32)]
    slice x10 -> x1, local copies, waits for them, and re-layouts: 4.07 us -> 0.01 us  [on_device(): open_cells[depth - SWEEPS:]]
  transfers between devices with their start and end apart: 7 -> 12, of which waited for: 7 -> 9; matrix products, arithmetic and copies ran while one was open for 1% -> 0% of each run, Pallas kernels for 0% -> 0%
where the time goes in v1:
time: 73.9 us; the launch traced here: 73.6 us
  waiting for transfers between devices  29.3 us (40%)
  Pallas kernels  20.2 us (27%)
  starting transfers between devices  19.5 us (26%)
  other arithmetic  2.07 us (3%)
  local copies, waits for them, and re-layouts  1.69 us (2%)
  between operations  0.78 us (1%)
    ppermute x5, waiting for transfers between devices, exchanged(): lax.ppermute(block, axis, [(i, i ^ bit) for i in range(lax.axis_size(axis...  22.2 us
    ppermute x7, starting transfers between devices, moved(): lax.ppermute(block, axis, [(i - distance, i) for i in devices if i - dist...  14.5 us
    pallas_call x1, Pallas kernels, solve(): pl.pallas_call(functools.partial(solve_kernel, depth, total_depth), grid=...  10.8 us
    ppermute x7, waiting for transfers between devices, moved(): lax.ppermute(block, axis, [(i - distance, i) for i in devices if i - dist...  7.08 us
    ppermute x5, starting transfers between devices, exchanged(): lax.ppermute(block, axis, [(i, i ^ bit) for i in range(lax.axis_size(axis...  5.04 us
    pallas_call x1, Pallas kernels, analyse(): pl.pallas_call(analyse_kernel, grid=(len(tiles),), in_specs=[pl.BlockSpec...  4.31 us
    pallas_call x1, Pallas kernels, synthesise(): pl.pallas_call(functools.partial(synthesise_kernel, len(pieces)), grid=(d...  4.06 us
    unnamed x6, local copies, waits for them, and re-layouts  1.6 us
  transfers between devices with their start and end apart: 12, of which 9 were waited for; matrix products, arithmetic and copies ran while one was open for 0% of the time, Pallas kernels for 0%

profile of v1, /device:TPU:0, one launch (start us, length us, event | category | flops | bytes accessed | tf_op | source)
XLA Modules:
  0.0 73.6 jit_solution(5028846592571061528)
XLA Ops:
  0.6 0.7 and_select_fusion
  1.3 0.7 %select_reduce_fusion = s32[128]{0:T(128)S(1)} fusion(s32[64]{0:T(128)} %param.6, s32[128]{0:T(128)S(1)} %get-tuple-element.18), kind=kLoop, calls=%fused_computation.28 | loop fusion | flops 24448 | bytes 1280 | tf_op jit(solution)/shard_map/reduce_sum | solution.py:266
  2.1 0.2 fusion.1.basis_ref
  2.3 4.3 %analyse.1 = (f32[32,64,256]{2,1,0:T(8,128)S(1)}, f32[32,64,256]{2,1,0:T(8,128)S(1)}) custom-call(bf16[256,32,256]{2,1,0:T(8,128)(2,1)} %charge_ref.1, bf16[128,256]{1,0:T(8,128)(2,1)S(1)} %fusion.1.basis_ref), custom_call_target="tpu_custom_call" | custom-call | tf_op jit(solution)/shard_map/analyse/pallas_call | solution.py:70
  6.6 0.6 collective-permute-start
  7.2 3.8 %collective-permute-done.recv_ref = f32[32,64,256]{2,1,0:T(8,128)S(1)} collective-permute-done((f32[32,64,256]{2,1,0:T(8,128)S(1)}, f32[32,64,256]{2,1,0:T(8,128)S(1)}, u32[]{:S(2)}, u32[]{:S(2)}) %collective-permute-start) | collective-permute-done | bytes 2097184 | tf_op jit(solution)/shard_map/ppermute | solution.py:234
  11.0 0.0 copy-start
  11.0 0.0 copy-start.2
  11.0 1.0 %round_sums.1 = (bf16[32,32,256]{2,1,0:T(8,128)(2,1)S(1)}, f32[32,256]{1,0:T(8,128)}) custom-call(f32[32,64,256]{2,1,0:T(8,128)S(1)} %get-tuple-element.8.keep_ref, f32[32,64,256]{2,1,0:T(8,128)S(1)} %collective-permute-done.recv_ref, f32[32,256]{1,0:T(8,128)S(1)} %broadcast_in_dim.62.state_ref), custom_call_target="tpu_custom_call" | custom-call | tf_op jit(solution)/shard_map/round_sums/pallas_call | solution.py:102
  12.0 2.9 %collective-permute-start.1 = (bf16[32,32,256]{2,1,0:T(8,128)(2,1)S(1)}, bf16[32,32,256]{2,1,0:T(8,128)(2,1)S(1)}, u32[]{:S(2)}, u32[]{:S(2)}) collective-permute-start(bf16[32,32,256]{2,1,0:T(8,128)(2,1)S(1)} %get-tuple-element.10), channel_id=1, source_target_pairs={{0,2},{1,3},{2,0},{3,1},{4,6},{5,7},{6,4},{7,5},{8,10},{9,11},{10,... | collective-permute-start | bytes 1572872 | tf_op jit(solution)/shard_map/ppermute | solution.py:234
  14.9 0.0 copy-done.2
  14.9 3.5 %collective-permute-start.4 = (f32[4,256]{1,0:T(4,128)S(1)}, f32[4,256]{1,0:T(4,128)S(1)}, u32[]{:S(2)}, u32[]{:S(2)}) collective-permute-start(f32[4,256]{1,0:T(4,128)S(1)} %get-tuple-element.16), channel_id=1, source_target_pairs={{0,4},{4,8},{8,12},{1,5},{5,9},{9,13},{2,6},{6,10},{10,14},{3,7},{... | collective-permute-start | bytes 12296 | tf_op jit(solution)/shard_map/ppermute | solution.py:239
  18.4 1.3 %collective-permute-start.5 = (f32[4,256]{1,0:T(4,128)S(1)}, f32[4,256]{1,0:T(4,128)S(1)}, u32[]{:S(2)}, u32[]{:S(2)}) collective-permute-start(f32[4,256]{1,0:T(4,128)S(1)} %get-tuple-element.17), channel_id=1, source_target_pairs={{4,0},{8,4},{12,8},{5,1},{9,5},{13,9},{6,2},{10,6},{14,10},{7,3},{... | collective-permute-start | bytes 12296 | tf_op jit(solution)/shard_map/ppermute | solution.py:239
  19.7 7.4 %collective-permute-done.1.far_ref = bf16[32,32,256]{2,1,0:T(8,128)(2,1)S(1)} collective-permute-done((bf16[32,32,256]{2,1,0:T(8,128)(2,1)S(1)}, bf16[32,32,256]{2,1,0:T(8,128)(2,1)S(1)}, u32[]{:S(2)}, u32[]{:S(2)}) %collective-permute-start.1) | collective-permute-done | bytes 524320 | tf_op jit(solution)/shard_map/ppermute | solution.py:234
  27.1 0.0 copy-done
  27.1 1.3 %collective-permute-start.3 = (f32[4,32,256]{2,1,0:T(8,128)S(1)}, f32[4,32,256]{2,1,0:T(8,128)S(1)}, u32[]{:S(2)}, u32[]{:S(2)}) collective-permute-start(f32[4,32,256]{2,1,0:T(8,128)S(1)} %get-tuple-element.14), channel_id=1, source_target_pairs={{4,0},{8,4},{12,8},{5,1},{9,5},{13,9},{6,2},{10,6},{14,10},{7,3},{... | collective-permute-start | bytes 393224 | tf_op jit(solution)/shard_map/ppermute | solution.py:239
  28.4 4.6 %collective-permute-start.2 = (f32[4,32,256]{2,1,0:T(8,128)S(1)}, f32[4,32,256]{2,1,0:T(8,128)S(1)}, u32[]{:S(2)}, u32[]{:S(2)}) collective-permute-start(f32[4,32,256]{2,1,0:T(8,128)S(1)} %get-tuple-element.15), channel_id=1, source_target_pairs={{0,4},{4,8},{8,12},{1,5},{5,9},{9,13},{2,6},{6,10},{10,14},{3,7},{... | collective-permute-start | bytes 393224 | tf_op jit(solution)/shard_map/ppermute | solution.py:239
  33.0 0.1 copy.8.order_ref
  33.1 0.0 collective-permute-done.4
  33.1 0.0 collective-permute-done.5
  33.1 0.9 %collective-permute-done.3.after_ref = f32[4,32,256]{2,1,0:T(8,128)S(1)} collective-permute-done((f32[4,32,256]{2,1,0:T(8,128)S(1)}, f32[4,32,256]{2,1,0:T(8,128)S(1)}, u32[]{:S(2)}, u32[]{:S(2)}) %collective-permute-start.3) | collective-permute-done | bytes 131104 | tf_op jit(solution)/shard_map/ppermute | solution.py:239
  34.0 1.5 %collective-permute-done.2.before_ref = f32[4,32,256]{2,1,0:T(8,128)S(1)} collective-permute-done((f32[4,32,256]{2,1,0:T(8,128)S(1)}, f32[4,32,256]{2,1,0:T(8,128)S(1)}, u32[]{:S(2)}, u32[]{:S(2)}) %collective-permute-start.2) | collective-permute-done | bytes 131104 | tf_op jit(solution)/shard_map/ppermute | solution.py:239
  35.5 0.0 copy-start.1
  35.5 1.6 %copy-done.1 = f32[32,64,256]{2,1,0:T(8,128)S(1)} copy-done((f32[32,64,256]{2,1,0:T(8,128)S(1)}, f32[32,64,256]{2,1,0:T(8,128)}, u32[]{:S(2)}) %copy-start.1) | copy-done | bytes 2097176
  37.1 10.8 %solve.1 = (f32[32,32,256]{2,1,0:T(8,128)}, f32[32,32,256]{2,1,0:T(8,128)S(1)}, f32[32,256]{1,0:T(8,128)S(1)}) custom-call(f32[32,64,256]{2,1,0:T(8,128)S(1)} %get-tuple-element.8.keep_ref, f32[32,64,256]{2,1,0:T(8,128)S(1)} %copy-done.1, bf16[32,32,256]{2,1,0:T(8,128)(2,1)S(1)} %collective-permute-done.1.far_ref, ...), custom_call_target="tpu_custom_call" | custom-call | tf_op jit(solution)/shard_map/solve/pallas_call | solution.py:184
  47.9 1.3 %collective-permute-start.8 = (f32[32,256]{1,0:T(8,128)S(1)}, f32[32,256]{1,0:T(8,128)S(1)}, u32[]{:S(2)}, u32[]{:S(2)}) collective-permute-start(f32[32,256]{1,0:T(8,128)S(1)} %get-tuple-element.12), channel_id=1, source_target_pairs={{12,0},{13,1},{14,2},{15,3},{28,16},{29,17},{30,18},{31,19}} | collective-permute-start | bytes 98312 | tf_op jit(solution)/shard_map/ppermute | solution.py:239
  49.2 1.3 %collective-permute-start.7 = (f32[32,256]{1,0:T(8,128)S(1)}, f32[32,256]{1,0:T(8,128)S(1)}, u32[]{:S(2)}, u32[]{:S(2)}) collective-permute-start(f32[32,256]{1,0:T(8,128)S(1)} %get-tuple-element.12), channel_id=1, source_target_pairs={{8,0},{12,4},{9,1},{13,5},{10,2},{14,6},{11,3},{15,7},{24,16},{28,... | collective-permute-start | bytes 98312 | tf_op jit(solution)/shard_map/ppermute | solution.py:239
  50.5 1.3 %collective-permute-start.6 = (f32[32,256]{1,0:T(8,128)S(1)}, f32[32,256]{1,0:T(8,128)S(1)}, u32[]{:S(2)}, u32[]{:S(2)}) collective-permute-start(f32[32,256]{1,0:T(8,128)S(1)} %get-tuple-element.12), channel_id=1, source_target_pairs={{4,0},{8,4},{12,8},{5,1},{9,5},{13,9},{6,2},{10,6},{14,10},{7,3},{... | collective-permute-start | bytes 98312 | tf_op jit(solution)/shard_map/ppermute | solution.py:239
  51.8 4.0 %collective-permute-done.8 = f32[32,256]{1,0:T(8,128)S(1)} collective-permute-done((f32[32,256]{1,0:T(8,128)S(1)}, f32[32,256]{1,0:T(8,128)S(1)}, u32[]{:S(2)}, u32[]{:S(2)}) %collective-permute-start.8) | collective-permute-done | bytes 32800 | tf_op jit(solution)/shard_map/ppermute | solution.py:239
  55.8 0.3 collective-permute-done.7
  56.2 0.3 collective-permute-done.6
  56.5 0.1 add_convert_fusion.refs_0_
  56.6 1.6 %collective-permute-start.9 = (bf16[32,32,256]{2,1,0:T(8,128)(2,1)S(1)}, bf16[32,32,256]{2,1,0:T(8,128)(2,1)S(1)}, u32[]{:S(2)}, u32[]{:S(2)}) collective-permute-start(bf16[32,32,256]{2,1,0:T(8,128)(2,1)S(1)} %add_convert_fusion.refs_0_), channel_id=1, source_target_pairs={{0,2},{1,3},{2,0},{3,1},{4,6},{5,7},{6,4},{7,5},{8,10},{9,11},{10,... | collective-permute-start | bytes 1572872 | tf_op jit(solution)/shard_map/ppermute | solution.py:234
  58.3 0.0 collective-permute-start.10
  58.3 9.3 %collective-permute-done.9.refs_1_ = bf16[32,32,256]{2,1,0:T(8,128)(2,1)S(1)} collective-permute-done((bf16[32,32,256]{2,1,0:T(8,128)(2,1)S(1)}, bf16[32,32,256]{2,1,0:T(8,128)(2,1)S(1)}, u32[]{:S(2)}, u32[]{:S(2)}) %collective-permute-start.9) | collective-permute-done | bytes 524320 | tf_op jit(solution)/shard_map/ppermute | solution.py:234
  67.6 0.0 collective-permute-start.11
  67.6 0.2 fusion.3.refs_4_
  67.8 0.0 collective-permute-done.10.refs_2_
  67.8 1.7 %collective-permute-done.11.refs_3_ = bf16[32,32,256]{2,1,0:T(8,128)(2,1)S(1)} collective-permute-done((bf16[32,32,256]{2,1,0:T(8,128)(2,1)S(1)}, bf16[32,32,256]{2,1,0:T(8,128)(2,1)S(1)}, u32[]{:S(2)}, u32[]{:S(2)}) %collective-permute-start.11) | collective-permute-done | bytes 524320 | tf_op jit(solution)/shard_map/ppermute | solution.py:234
  69.5 4.1 %synthesise.1 = bf16[256,32,256]{2,1,0:T(8,128)(2,1)} custom-call(bf16[32,32,256]{2,1,0:T(8,128)(2,1)S(1)} %add_convert_fusion.refs_0_, bf16[32,32,256]{2,1,0:T(8,128)(2,1)S(1)} %collective-permute-done.9.refs_1_, bf16[32,32,256]{2,1,0:T(8,128)(2,1)S(1)} %collective-permute-done.10.refs_2_, bf16[32,32,256]{2,1,0:T(8,128)(2,1)S(1)} %collective-permute-done.11.refs_3_, ...), custom_call_target="tpu_custom_call" | custom-call | tf_op jit(solution)/shard_map/synthesise/pallas_call | solution.py:220
  (8 shorter events, 0.1 us)
Async XLA Ops:
  6.6 4.3 %collective-permute-start = (f32[32,64,256]{2,1,0:T(8,128)S(1)}, f32[32,64,256]{2,1,0:T(8,128)S(1)}, u32[]{:S(2)}, u32[]{:S(2)}) collective-permute-start(f32[32,64,256]{2,1,0:T(8,128)S(1)} %get-tuple-element.9), channel_id=1, source_target_pairs={{0,1},{1,0},{2,3},{3,2},{4,5},{5,4},{6,7},{7,6},{8,9},{9,8},{10,11... | collective-permute-start | bytes 6291464 | tf_op jit(solution)/shard_map/ppermute | solution.py:234
  11.0 16.1 %copy-start = (f32[32,64,256]{2,1,0:T(8,128)}, f32[32,64,256]{2,1,0:T(8,128)S(1)}, u32[]{:S(2)}) copy-start(f32[32,64,256]{2,1,0:T(8,128)S(1)} %collective-permute-done.recv_ref) | copy-start | bytes 6291460
  11.0 3.9 %copy-start.2 = (s32[32,256]{1,0:T(8,128)S(1)}, s32[32,256]{1,0:T(8,128)}, u32[]{:S(2)}) copy-start(s32[32,256]{1,0:T(8,128)} %param.7) | copy-start | bytes 98308
  12.0 15.1 %collective-permute-start.1 = (bf16[32,32,256]{2,1,0:T(8,128)(2,1)S(1)}, bf16[32,32,256]{2,1,0:T(8,128)(2,1)S(1)}, u32[]{:S(2)}, u32[]{:S(2)}) collective-permute-start(bf16[32,32,256]{2,1,0:T(8,128)(2,1)S(1)} %get-tuple-element.10), channel_id=1, source_target_pairs={{0,2},{1,3},{2,0},{3,1},{4,6},{5,7},{6,4},{7,5},{8,10},{9,11},{10,... | collective-permute-start | bytes 1572872 | tf_op jit(solution)/shard_map/ppermute | solution.py:234
  14.9 18.2 %collective-permute-start.4 = (f32[4,256]{1,0:T(4,128)S(1)}, f32[4,256]{1,0:T(4,128)S(1)}, u32[]{:S(2)}, u32[]{:S(2)}) collective-permute-start(f32[4,256]{1,0:T(4,128)S(1)} %get-tuple-element.16), channel_id=1, source_target_pairs={{0,4},{4,8},{8,12},{1,5},{5,9},{9,13},{2,6},{6,10},{10,14},{3,7},{... | collective-permute-start | bytes 12296 | tf_op jit(solution)/shard_map/ppermute | solution.py:239
  18.4 14.7 %collective-permute-start.5 = (f32[4,256]{1,0:T(4,128)S(1)}, f32[4,256]{1,0:T(4,128)S(1)}, u32[]{:S(2)}, u32[]{:S(2)}) collective-permute-start(f32[4,256]{1,0:T(4,128)S(1)} %get-tuple-element.17), channel_id=1, source_target_pairs={{4,0},{8,4},{12,8},{5,1},{9,5},{13,9},{6,2},{10,6},{14,10},{7,3},{... | collective-permute-start | bytes 12296 | tf_op jit(solution)/shard_map/ppermute | solution.py:239
  27.1 6.9 %collective-permute-start.3 = (f32[4,32,256]{2,1,0:T(8,128)S(1)}, f32[4,32,256]{2,1,0:T(8,128)S(1)}, u32[]{:S(2)}, u32[]{:S(2)}) collective-permute-start(f32[4,32,256]{2,1,0:T(8,128)S(1)} %get-tuple-element.14), channel_id=1, source_target_pairs={{4,0},{8,4},{12,8},{5,1},{9,5},{13,9},{6,2},{10,6},{14,10},{7,3},{... | collective-permute-start | bytes 393224 | tf_op jit(solution)/shard_map/ppermute | solution.py:239
  28.4 7.1 %collective-permute-start.2 = (f32[4,32,256]{2,1,0:T(8,128)S(1)}, f32[4,32,256]{2,1,0:T(8,128)S(1)}, u32[]{:S(2)}, u32[]{:S(2)}) collective-permute-start(f32[4,32,256]{2,1,0:T(8,128)S(1)} %get-tuple-element.15), channel_id=1, source_target_pairs={{0,4},{4,8},{8,12},{1,5},{5,9},{9,13},{2,6},{6,10},{10,14},{3,7},{... | collective-permute-start | bytes 393224 | tf_op jit(solution)/shard_map/ppermute | solution.py:239
  35.5 1.6 %copy-start.1 = (f32[32,64,256]{2,1,0:T(8,128)S(1)}, f32[32,64,256]{2,1,0:T(8,128)}, u32[]{:S(2)}) copy-start(f32[32,64,256]{2,1,0:T(8,128)} %copy-done) | copy-start | bytes 6291460
  47.9 7.9 %collective-permute-start.8 = (f32[32,256]{1,0:T(8,128)S(1)}, f32[32,256]{1,0:T(8,128)S(1)}, u32[]{:S(2)}, u32[]{:S(2)}) collective-permute-start(f32[32,256]{1,0:T(8,128)S(1)} %get-tuple-element.12), channel_id=1, source_target_pairs={{12,0},{13,1},{14,2},{15,3},{28,16},{29,17},{30,18},{31,19}} | collective-permute-start | bytes 98312 | tf_op jit(solution)/shard_map/ppermute | solution.py:239
  49.2 7.0 %collective-permute-start.7 = (f32[32,256]{1,0:T(8,128)S(1)}, f32[32,256]{1,0:T(8,128)S(1)}, u32[]{:S(2)}, u32[]{:S(2)}) collective-permute-start(f32[32,256]{1,0:T(8,128)S(1)} %get-tuple-element.12), channel_id=1, source_target_pairs={{8,0},{12,4},{9,1},{13,5},{10,2},{14,6},{11,3},{15,7},{24,16},{28,... | collective-permute-start | bytes 98312 | tf_op jit(solution)/shard_map/ppermute | solution.py:239
  50.5 6.0 %collective-permute-start.6 = (f32[32,256]{1,0:T(8,128)S(1)}, f32[32,256]{1,0:T(8,128)S(1)}, u32[]{:S(2)}, u32[]{:S(2)}) collective-permute-start(f32[32,256]{1,0:T(8,128)S(1)} %get-tuple-element.12), channel_id=1, source_target_pairs={{4,0},{8,4},{12,8},{5,1},{9,5},{13,9},{6,2},{10,6},{14,10},{7,3},{... | collective-permute-start | bytes 98312 | tf_op jit(solution)/shard_map/ppermute | solution.py:239
  56.6 11.0 %collective-permute-start.9 = (bf16[32,32,256]{2,1,0:T(8,128)(2,1)S(1)}, bf16[32,32,256]{2,1,0:T(8,128)(2,1)S(1)}, u32[]{:S(2)}, u32[]{:S(2)}) collective-permute-start(bf16[32,32,256]{2,1,0:T(8,128)(2,1)S(1)} %add_convert_fusion.refs_0_), channel_id=1, source_target_pairs={{0,2},{1,3},{2,0},{3,1},{4,6},{5,7},{6,4},{7,5},{8,10},{9,11},{10,... | collective-permute-start | bytes 1572872 | tf_op jit(solution)/shard_map/ppermute | solution.py:234
  58.3 9.6 %collective-permute-start.10 = (bf16[32,32,256]{2,1,0:T(8,128)(2,1)S(1)}, bf16[32,32,256]{2,1,0:T(8,128)(2,1)S(1)}, u32[]{:S(2)}, u32[]{:S(2)}) collective-permute-start(bf16[32,32,256]{2,1,0:T(8,128)(2,1)S(1)} %add_convert_fusion.refs_0_), channel_id=1, source_target_pairs={{0,1},{1,0},{2,3},{3,2},{4,5},{5,4},{6,7},{7,6},{8,9},{9,8},{10,11... | collective-permute-start | bytes 1572872 | tf_op jit(solution)/shard_map/ppermute | solution.py:234
  67.6 1.9 %collective-permute-start.11 = (bf16[32,32,256]{2,1,0:T(8,128)(2,1)S(1)}, bf16[32,32,256]{2,1,0:T(8,128)(2,1)S(1)}, u32[]{:S(2)}, u32[]{:S(2)}) collective-permute-start(bf16[32,32,256]{2,1,0:T(8,128)(2,1)S(1)} %collective-permute-done.9.refs_1_), channel_id=1, source_target_pairs={{0,1},{1,0},{2,3},{3,2},{4,5},{5,4},{6,7},{7,6},{8,9},{9,8},{10,11... | collective-permute-start | bytes 1572872 | tf_op jit(solution)/shard_map/ppermute | solution.py:234
